TPU v7x, 32 devices: a whole 2x2x4 slice. The times are simulated.
32 devices in a mesh: pos: 8 (over y, x, core), ang: 4 (over z).
Axes of the slice: x: 2, y: 2, z: 4, core: 2. Of those that a mesh axis runs over, the one named last changes fastest.
Arguments:
- object_field: float32 [2, 32, 256, 256], P(None, None, 'pos'), may hold values from -2.5 to 2.5
- probe_wave: float32 [2, 128, 128], replicated, may hold values from -4 to 4
- intensity: float32 [4, 32, 128, 128], P('ang', 'pos'), may hold values from 0.25 to 4
- positions: int32 [32, 2], P('pos'), may hold values from 0 to 255, as said below
- shear_steps: int32 [4, 32], replicated, may hold values from -8 to 8, as said below
Outputs:
- object_new: float32 [2, 32, 256, 256], P(None, None, 'pos')
Inputs may be any that keep to these rules, and one draw needn't show every extreme that they name: `positions`: row j is (column offset, row offset). With d = j // 4 and q = j mod 4: (column offset - d * 32 + 128 // 2) mod 256 lies in 0 .. 32; it is 0 for q = 0 and 32 for q = 1; the row offset lies in 0 .. 128, and is 128 for q = 0 and 0 for q = 1. For every angle a, shear_steps[a, 0] = -8 and shear_steps[a, 31] = 8.
All inputs are finite; a program needn't handle non-finite values.
Results may differ from a plain program's by a relative error of at most 0.0001.
Values sent between devices are 32-bit elements; how exact they have to be, the bound alone decides.
A program may use at most 64 MiB of HBM per device.

v0:
```python
import math

import jax
import jax.numpy as jnp
from jax import lax
from jax.sharding import PartitionSpec as P

FRAME = 128
Y = 256
SH = 8
ITERS = 3


MODULUS_FLOOR = 0.25
INTERSECTION_WEIGHT = 1.0
RELAXATION = 0.5
HIGHEST = lax.Precision.HIGHEST


def padded_2(block, sides, width):
    for axis, dim in sides:
        count = lax.axis_size(axis)
        forward = [(i, i + 1) for i in range(count - 1)]
        forward.append((count - 1, 0))
        backward = [(target, source) for source, target in forward]
        low = lax.ppermute(
            lax.slice_in_dim(block, block.shape[dim] - width, None, axis=dim), axis, forward
        )
        high = lax.ppermute(lax.slice_in_dim(block, 0, width, axis=dim), axis, backward)
        block = jnp.concatenate([low, block, high], axis=dim)
    return block


def passed_along(value, axis, steps):
    count = lax.axis_size(axis)
    pairs = [(source, (source + steps) % count) for source in range(count)]
    return lax.ppermute(value, axis, pairs)


def fourier_tables(length):
    indices = jnp.arange(length, dtype=jnp.int32)
    phases = (indices[:, None] * indices[None, :] % length).astype(jnp.float32) * (
        2.0 * math.pi / length
    )
    factor = 1.0 / math.sqrt(length)
    return (jnp.cos(phases) * factor, jnp.sin(phases) * factor)


def transform(real_part, imag_part, cosine, sine_table, exponent_sign):
    left_real = jnp.einsum(
        "jk,abkl->abjl", cosine, real_part, precision=HIGHEST
    ) - exponent_sign * jnp.einsum("jk,abkl->abjl", sine_table, imag_part, precision=HIGHEST)
    left_imag = jnp.einsum(
        "jk,abkl->abjl", cosine, imag_part, precision=HIGHEST
    ) + exponent_sign * jnp.einsum("jk,abkl->abjl", sine_table, real_part, precision=HIGHEST)
    out_real = jnp.einsum(
        "abjk,kl->abjl", left_real, cosine, precision=HIGHEST
    ) - exponent_sign * jnp.einsum("abjk,kl->abjl", left_imag, sine_table, precision=HIGHEST)
    out_imag = jnp.einsum(
        "abjk,kl->abjl", left_imag, cosine, precision=HIGHEST
    ) + exponent_sign * jnp.einsum("abjk,kl->abjl", left_real, sine_table, precision=HIGHEST)
    return (out_real, out_imag)


def deposit(target, get_piece, start_cols, start_rows, frame_total):
    leading = target.ndim - 2

    def add_one(frame_index, running):
        corner = (0,) * leading + (start_cols[frame_index], start_rows[frame_index])
        addition = get_piece(frame_index)
        current = lax.dynamic_slice(running, corner, addition.shape)
        return lax.dynamic_update_slice(running, current + addition, corner)

    return lax.fori_loop(0, frame_total, add_one, target)


def extract(source, start_cols, start_rows):
    leading = source.shape[:-2]

    def window_at(col_start, row_start):
        return lax.dynamic_slice(
            source, (0,) * len(leading) + (col_start, row_start), leading + (FRAME, FRAME)
        )

    return jax.vmap(window_at, out_axes=2)(start_cols, start_rows)


def per_device(object_field, probe_wave, intensity, positions, shear_steps):
    tile_width = object_field.shape[2]
    full_width = tile_width * lax.axis_size("pos")
    pos_index = lax.axis_index("pos")
    angle_count = intensity.shape[0]
    frame_total = positions.shape[0]
    angle_first = lax.axis_index("ang") * angle_count
    reach_tiles = -(-(FRAME // 2) // tile_width)
    band_count = 2 * reach_tiles + 1
    padded_width = tile_width + 2 * SH
    columns = jnp.arange(tile_width, dtype=jnp.int32)
    padded_cols = jnp.arange(padded_width, dtype=jnp.int32)
    my_steps = lax.dynamic_slice_in_dim(shear_steps, angle_first, angle_count, 0)
    padded = padded_2(object_field, (("pos", 2),), SH)
    forward_pick = (
        padded_cols[None, None, None, :]
        == columns[None, None, :, None] + SH + my_steps[:, :, None, None]
    ).astype(jnp.float32)
    projected = jnp.einsum("azxk,czky->acxy", forward_pick, padded, precision=HIGHEST)
    start_rows = positions[:, 1]
    start_cols = (positions[:, 0] - pos_index * tile_width + reach_tiles * tile_width) % full_width
    work_width = band_count * tile_width
    probe_real = probe_wave[0]
    probe_imag = probe_wave[1]
    probe_power = probe_real * probe_real + probe_imag * probe_imag
    cover_plane = deposit(
        jnp.zeros((work_width, Y), jnp.float32),
        lambda frame_index: probe_power,
        start_cols,
        start_rows,
        frame_total,
    )
    coverage = cover_plane[reach_tiles * tile_width : (reach_tiles + 1) * tile_width]
    for offset in range(band_count):
        if offset != reach_tiles:
            coverage = coverage + passed_along(
                cover_plane[offset * tile_width : (offset + 1) * tile_width],
                "pos",
                offset - reach_tiles,
            )
    cosine, sine_table = fourier_tables(FRAME)
    amplitude = jnp.sqrt(intensity)
    estimate = projected
    for iteration in range(ITERS):
        pieces = []
        for offset in range(band_count):
            if offset == reach_tiles:
                pieces.append(estimate)
            else:
                pieces.append(passed_along(estimate, "pos", reach_tiles - offset))
        source = jnp.concatenate(pieces, axis=2)
        patches = extract(source, start_cols, start_rows)
        patch_real = patches[:, 0]
        patch_imag = patches[:, 1]
        wave_real = probe_real * patch_real - probe_imag * patch_imag
        wave_imag = probe_real * patch_imag + probe_imag * patch_real
        freq_real, freq_imag = transform(wave_real, wave_imag, cosine, sine_table, -1.0)
        modulus = jnp.sqrt(freq_real * freq_real + freq_imag * freq_imag)
        factor = amplitude / jnp.maximum(modulus, MODULUS_FLOOR)
        exit_real, exit_imag = transform(
            freq_real * factor, freq_imag * factor, cosine, sine_table, 1.0
        )
        back_real = probe_real * exit_real + probe_imag * exit_imag
        back_imag = probe_real * exit_imag - probe_imag * exit_real
        contrib = jnp.stack([back_real, back_imag], axis=1)
        summed = deposit(
            jnp.zeros((angle_count, 2, work_width, Y), jnp.float32),
            lambda frame_index: contrib[:, :, frame_index],
            start_cols,
            start_rows,
            frame_total,
        )
        numerator = summed[:, :, reach_tiles * tile_width : (reach_tiles + 1) * tile_width]
        for offset in range(band_count):
            if offset != reach_tiles:
                numerator = numerator + passed_along(
                    summed[:, :, offset * tile_width : (offset + 1) * tile_width],
                    "pos",
                    offset - reach_tiles,
                )
        estimate = (numerator + INTERSECTION_WEIGHT * estimate) / (coverage + INTERSECTION_WEIGHT)
    change = estimate - projected
    change_rim = padded_2(change, (("pos", 2),), SH)
    every_rim = lax.all_gather(change_rim, "ang", axis=0, tiled=True)
    back_pick = (
        padded_cols[None, None, None, :]
        == columns[None, None, :, None] + SH - shear_steps[:, :, None, None]
    ).astype(jnp.float32)
    accumulated = jnp.einsum("azxk,acky->czxy", back_pick, every_rim, precision=HIGHEST)
    return object_field + RELAXATION / shear_steps.shape[0] * accumulated


def solution(mesh):
    placed = (P(None, None, "pos", None), P(), P("ang", "pos", None, None), P("pos", None), P())
    return jax.shard_map(
        per_device,
        mesh=mesh,
        in_specs=placed,
        out_specs=P(None, None, "pos", None),
        check_vma=False,
    )
```

profile of v0, /device:TPU:0, one launch (start us, length us, event | category | flops | bytes accessed | tf_op | source)
XLA Modules:
  0.0 268.8 jit_solution(3598538774012352433)
XLA Ops:
  0.0 2.3 fusion.380
  2.8 2.9 %collective-permute-start.1 = (f32[2,32,8,256]{3,2,1,0:T(8,128)S(1)}, f32[2,32,8,256]{3,2,1,0:T(8,128)}, u32[]{:S(2)}, u32[]{:S(2)}) collective-permute-start(f32[2,32,8,256]{3,2,1,0:T(8,128)S(1)} %get-tuple-element.525), channel_id=1, source_target_pairs={{4,0},{8,4},{12,8},{16,12},{20,16},{24,20},{28,24},{0,28},{5,1},{9... | collective-permute-start | bytes 1572872 | tf_op jit(solution)/shard_map/ppermute | solution.py:29
  6.8 25.7 %while.56 = (s32[]{:T(128)}, f32[160,256]{1,0:T(8,128)S(1)}, s32[4]{0:T(128)S(1)}, s32[4]{0:T(128)S(1)}, f32[128,128]{1,0:T(8,128)S(1)}, /*index=5*/s32[]{:T(128)}, s32[]{:T(128)}, s32[]{:T(128)}, s32[]{:T(128)}) while((s32[]{:T(128)}, f32[160,256]{1,0:T(8,128)S(1)}, s32[4]{0:T(128)S(1)}, s32[4]{0:T(128)S(1)}, f32[128,128]{1,0:T(8,128)S(1)}, ...), condition=%wide.region_3.4_spmd, body=%wide.region_2.3_spmd.sunk | while | flops 16392 | bytes 327877 | solution.py:74
  24.0 1.7 dynamic_update_slice.33
  30.7 1.7 dynamic_update_slice.33
  33.2 2.2 collective-permute-start.10
  36.2 2.5 fusion.35
  38.8 2.0 collective-permute-start.2
  40.9 3.5 %collective-permute-done.2 = f32[1,2,32,256]{3,2,1,0:T(8,128)S(1)} collective-permute-done((f32[1,2,32,256]{3,2,1,0:T(8,128)S(1)}, f32[1,2,32,256]{3,2,1,0:T(8,128)S(1)}, u32[]{:S(2)}, u32[]{:S(2)}) %collective-permute-start.2) | collective-permute-done | bytes 65568 | tf_op jit(solution)/shard_map/ppermute | solution.py:37
  44.5 4.4 %collective-permute-done.3 = f32[1,2,32,256]{3,2,1,0:T(8,128)S(1)} collective-permute-done((f32[1,2,32,256]{3,2,1,0:T(8,128)S(1)}, f32[1,2,32,256]{3,2,1,0:T(8,128)S(1)}, u32[]{:S(2)}, u32[]{:S(2)}) %collective-permute-start.3) | collective-permute-done | bytes 65568 | tf_op jit(solution)/shard_map/ppermute | solution.py:37
  49.0 1.9 collective-permute-done.4
  51.6 3.5 %collective-permute-done.5 = f32[1,2,32,256]{3,2,1,0:T(8,128)S(1)} collective-permute-done((f32[1,2,32,256]{3,2,1,0:T(8,128)S(1)}, f32[1,2,32,256]{3,2,1,0:T(8,128)S(1)}, u32[]{:S(2)}, u32[]{:S(2)}) %collective-permute-start.5) | collective-permute-done | bytes 65568 | tf_op jit(solution)/shard_map/ppermute | solution.py:37
  55.2 8.4 %while.59 = (s32[]{:T(128)}, f32[1,2,160,256]{3,2,1,0:T(8,128)S(1)}, s32[4,4]{1,0:T(4,128)S(1)}, f32[4,1,2,128,128]{4,3,0,2,1:T(8,128)S(1)}, s32[]{:T(128)}) while((s32[]{:T(128)}, f32[1,2,160,256]{3,2,1,0:T(8,128)S(1)}, s32[4,4]{1,0:T(4,128)S(1)}, f32[4,1,2,128,128]{4,3,0,2,1:T(8,128)S(1)}, s32[]{:T(128)}) %tuple.172), condition=%wide.while_cond, body=%wide.while_body.sunk | while | flops 2 | bytes 262269 | solution.py:81
  55.9 1.4 bitcast_dynamic-update-slice_fusion.6
  57.9 1.4 bitcast_dynamic-update-slice_fusion.6
  60.0 1.4 bitcast_dynamic-update-slice_fusion.6
  62.0 1.4 bitcast_dynamic-update-slice_fusion.6
  76.0 29.1 %while.55 = (s32[]{:T(128)}, f32[1,2,160,256]{3,2,1,0:T(8,128)S(1)}, s32[4]{0:T(128)S(1)}, s32[4]{0:T(128)S(1)}, f32[1,2,4,128,128]{4,3,2,1,0:T(8,128)S(1)}, /*index=5*/s32[]{:T(128)}, s32[]{:T(128)}, s32[]{:T(128)}, s32[]{:T(128)}) while((s32[]{:T(128)}, f32[1,2,160,256]{3,2,1,0:T(8,128)S(1)}, s32[4]{0:T(128)S(1)}, s32[4]{0:T(128)S(1)}, ...), condition=%wide.region_1.2_spmd, body=%wide.region_0.1_spmd.sunk | while | flops 32776 | bytes 655561 | solution.py:74
  95.2 2.2 dynamic_update_slice.32
  103.0 2.2 dynamic_update_slice.32
  105.2 1.6 collective-permute-start.6
  108.1 1.4 collective-permute-start.9
  110.3 2.5 collective-permute-done.8
  112.8 2.0 collective-permute-done.9
  114.9 2.6 collective-permute-start.16
  117.6 2.0 collective-permute-start.17
  120.3 1.8 collective-permute-done.17
  122.1 7.8 %while.60 = (s32[]{:T(128)}, f32[1,2,160,256]{3,2,1,0:T(8,128)S(1)}, s32[4,4]{1,0:T(4,128)S(1)}, f32[4,1,2,128,128]{4,3,0,2,1:T(8,128)S(1)}, s32[]{:T(128)}) while((s32[]{:T(128)}, f32[1,2,160,256]{3,2,1,0:T(8,128)S(1)}, s32[4,4]{1,0:T(4,128)S(1)}, f32[4,1,2,128,128]{4,3,0,2,1:T(8,128)S(1)}, s32[]{:T(128)}) %tuple.193), condition=%wide.while_cond.1, body=%wide.while_body.1.sunk | while | flops 2 | bytes 262269 | solution.py:81
  142.1 29.1 %while.57 = (s32[]{:T(128)}, f32[1,2,160,256]{3,2,1,0:T(8,128)S(1)}, s32[4]{0:T(128)S(1)}, s32[4]{0:T(128)S(1)}, f32[1,2,4,128,128]{4,3,2,1,0:T(8,128)S(1)}, /*index=5*/s32[]{:T(128)}, s32[]{:T(128)}, s32[]{:T(128)}, s32[]{:T(128)}) while((s32[]{:T(128)}, f32[1,2,160,256]{3,2,1,0:T(8,128)S(1)}, s32[4]{0:T(128)S(1)}, s32[4]{0:T(128)S(1)}, ...), condition=%wide.region_5.6_spmd, body=%wide.region_4.5_spmd.sunk | while | flops 32776 | bytes 655561 | solution.py:74
  161.3 2.2 dynamic_update_slice.34
  169.1 2.2 dynamic_update_slice.34
  171.3 2.6 collective-permute-start.18
  174.4 1.8 collective-permute-done.18
  178.5 1.4 collective-permute-done.21
  180.9 2.6 collective-permute-start.24
  185.9 1.9 collective-permute-done.25
  187.9 8.2 %while.61 = (s32[]{:T(128)}, f32[1,2,160,256]{3,2,1,0:T(8,128)S(1)}, s32[4,4]{1,0:T(4,128)S(1)}, f32[4,1,2,128,128]{4,3,0,2,1:T(8,128)S(1)}, s32[]{:T(128)}) while((s32[]{:T(128)}, f32[1,2,160,256]{3,2,1,0:T(8,128)S(1)}, s32[4,4]{1,0:T(4,128)S(1)}, f32[4,1,2,128,128]{4,3,0,2,1:T(8,128)S(1)}, s32[]{:T(128)}) %tuple.194), condition=%wide.while_cond.2, body=%wide.while_body.2.sunk | while | flops 2 | bytes 262269 | solution.py:81
  192.7 1.4 bitcast_dynamic-update-slice_fusion.8
  194.7 1.4 bitcast_dynamic-update-slice_fusion.8
  208.4 29.1 %while.58 = (s32[]{:T(128)}, f32[1,2,160,256]{3,2,1,0:T(8,128)S(1)}, s32[4]{0:T(128)S(1)}, s32[4]{0:T(128)S(1)}, f32[1,2,4,128,128]{4,3,2,1,0:T(8,128)S(1)}, /*index=5*/s32[]{:T(128)}, s32[]{:T(128)}, s32[]{:T(128)}, s32[]{:T(128)}) while((s32[]{:T(128)}, f32[1,2,160,256]{3,2,1,0:T(8,128)S(1)}, s32[4]{0:T(128)S(1)}, s32[4]{0:T(128)S(1)}, ...), condition=%wide.region_7.8_spmd, body=%wide.region_6.7_spmd.sunk | while | flops 32776 | bytes 655561 | solution.py:74
  227.5 2.2 dynamic_update_slice.35
  235.3 2.2 dynamic_update_slice.35
  237.5 2.0 collective-permute-start.26
  240.2 1.6 collective-permute-done.26
  244.1 1.4 collective-permute-done.29
  245.6 2.6 collective-permute-start.31
  249.7 15.3 %all_gather.3 = f32[4,2,48,256]{3,2,1,0:T(8,128)S(1)} all-gather(f32[1,2,48,256]{3,2,1,0:T(8,128)S(1)} %pad_maximum_fusion.3), channel_id=1, replica_groups=mesh['pos'=8,'ang'=4] {'ang'}, dimensions={0}, use_global_device_ids=true | all-gather | bytes 491520 | tf_op jit(solution)/shard_map/all_gather | solution.py:171
  265.0 3.6 %bitcast_add_fusion.3 = f32[2,32,32,256]{3,2,1,0:T(8,128)} fusion(f32[2,32,32,256]{3,2,1,0:T(8,128)S(1)} %copy-done, s32[4,32,32]{2,0,1:T(4,128)S(1)} %broadcast_subtract_fusion, f32[4,2,48,256]{3,2,1,0:T(8,128)S(1)} %all_gather.3), kind=kOutput, calls=%fused_computation.16 | convolution fusion | flops 1209204736 | bytes 4603904 | tf_op jit(solution)/shard_map/azxk,acky->czxy/dot_general | solution.py:176
  (244 shorter events, 101.4 us)
Async XLA Ops:
  0.0 36.2 %copy-start = (f32[2,32,32,256]{3,2,1,0:T(8,128)S(1)}, f32[2,32,32,256]{3,2,1,0:T(8,128)}, u32[]{:S(2)}) copy-start(f32[2,32,32,256]{3,2,1,0:T(8,128)} %param.13) | copy-start | bytes 6291460
  0.0 5.6 %copy-start.3 = (s32[4,2]{0,1:T(2,128)S(1)}, s32[4,2]{0,1:T(2,128)}, u32[]{:S(2)}) copy-start(s32[4,2]{0,1:T(2,128)} %param.16) | copy-start | bytes 100
  0.0 36.1 %copy-start.1 = (f32[2,128,128]{2,1,0:T(8,128)S(1)}, f32[2,128,128]{2,1,0:T(8,128)}, u32[]{:S(2)}) copy-start(f32[2,128,128]{2,1,0:T(8,128)} %param.14) | copy-start | bytes 393220
  0.0 36.0 %copy-start.2 = (s32[4,32]{1,0:T(4,128)S(1)}, s32[4,32]{1,0:T(4,128)}, u32[]{:S(2)}) copy-start(s32[4,32]{1,0:T(4,128)} %param.17) | copy-start | bytes 1540
  2.3 33.9 %collective-permute-start = (f32[2,32,8,256]{3,2,1,0:T(8,128)}, f32[2,32,8,256]{3,2,1,0:T(8,128)}, u32[]{:S(2)}, u32[]{:S(2)}) collective-permute-start(f32[2,32,8,256]{3,2,1,0:T(8,128)} %get-tuple-element.524), channel_id=1, source_target_pairs={{0,4},{4,8},{8,12},{12,16},{16,20},{20,24},{24,28},{28,0},{1,5},{5... | collective-permute-start | bytes 1572872 | tf_op jit(solution)/shard_map/ppermute | solution.py:26
  2.8 33.4 %collective-permute-start.1 = (f32[2,32,8,256]{3,2,1,0:T(8,128)S(1)}, f32[2,32,8,256]{3,2,1,0:T(8,128)}, u32[]{:S(2)}, u32[]{:S(2)}) collective-permute-start(f32[2,32,8,256]{3,2,1,0:T(8,128)S(1)} %get-tuple-element.525), channel_id=1, source_target_pairs={{4,0},{8,4},{12,8},{16,12},{20,16},{24,20},{28,24},{0,28},{5,1},{9... | collective-permute-start | bytes 1572872 | tf_op jit(solution)/shard_map/ppermute | solution.py:29
  33.2 73.7 %collective-permute-start.10 = (f32[32,256]{1,0:T(8,128)}, f32[32,256]{1,0:T(8,128)S(1)}, u32[]{:S(2)}, u32[]{:S(2)}) collective-permute-start(f32[32,256]{1,0:T(8,128)} %get-tuple-element.550), channel_id=1, source_target_pairs={{0,24},{4,28},{8,0},{12,4},{16,8},{20,12},{24,16},{28,20},{1,25},{... | collective-permute-start | bytes 98312 | tf_op jit(solution)/shard_map/ppermute | solution.py:37
  35.4 72.7 %collective-permute-start.11 = (f32[32,256]{1,0:T(8,128)}, f32[32,256]{1,0:T(8,128)S(1)}, u32[]{:S(2)}, u32[]{:S(2)}) collective-permute-start(f32[32,256]{1,0:T(8,128)} %get-tuple-element.553), channel_id=1, source_target_pairs={{0,28},{4,0},{8,4},{12,8},{16,12},{20,16},{24,20},{28,24},{1,29},{... | collective-permute-start | bytes 98312 | tf_op jit(solution)/shard_map/ppermute | solution.py:37
  35.4 72.7 %collective-permute-start.12 = (f32[32,256]{1,0:T(8,128)}, f32[32,256]{1,0:T(8,128)}, u32[]{:S(2)}, u32[]{:S(2)}) collective-permute-start(f32[32,256]{1,0:T(8,128)} %get-tuple-element.552), channel_id=1, source_target_pairs={{0,4},{4,8},{8,12},{12,16},{16,20},{20,24},{24,28},{28,0},{1,5},{5... | collective-permute-start | bytes 98312 | tf_op jit(solution)/shard_map/ppermute | solution.py:37
  36.1 73.3 %collective-permute-start.13 = (f32[32,256]{1,0:T(8,128)}, f32[32,256]{1,0:T(8,128)}, u32[]{:S(2)}, u32[]{:S(2)}) collective-permute-start(f32[32,256]{1,0:T(8,128)} %get-tuple-element.551), channel_id=1, source_target_pairs={{0,8},{4,12},{8,16},{12,20},{16,24},{20,28},{24,0},{28,4},{1,9},{5... | collective-permute-start | bytes 98312 | tf_op jit(solution)/shard_map/ppermute | solution.py:37
  38.8 5.6 %collective-permute-start.2 = (f32[1,2,32,256]{3,2,1,0:T(8,128)S(1)}, f32[1,2,32,256]{3,2,1,0:T(8,128)S(1)}, u32[]{:S(2)}, u32[]{:S(2)}) collective-permute-start(f32[1,2,32,256]{3,2,1,0:T(8,128)S(1)} %fusion.35), channel_id=1, source_target_pairs={{0,8},{4,12},{8,16},{12,20},{16,24},{20,28},{24,0},{28,4},{1,9},{5... | collective-permute-start | bytes 196616 | tf_op jit(solution)/shard_map/ppermute | solution.py:37
  44.4 4.6 %collective-permute-start.3 = (f32[1,2,32,256]{3,2,1,0:T(8,128)S(1)}, f32[1,2,32,256]{3,2,1,0:T(8,128)S(1)}, u32[]{:S(2)}, u32[]{:S(2)}) collective-permute-start(f32[1,2,32,256]{3,2,1,0:T(8,128)S(1)} %fusion.35), channel_id=1, source_target_pairs={{0,4},{4,8},{8,12},{12,16},{16,20},{20,24},{24,28},{28,0},{1,5},{5... | collective-permute-start | bytes 196616 | tf_op jit(solution)/shard_map/ppermute | solution.py:37
  49.0 1.9 collective-permute-start.4
  50.9 4.3 %collective-permute-start.5 = (f32[1,2,32,256]{3,2,1,0:T(8,128)S(1)}, f32[1,2,32,256]{3,2,1,0:T(8,128)S(1)}, u32[]{:S(2)}, u32[]{:S(2)}) collective-permute-start(f32[1,2,32,256]{3,2,1,0:T(8,128)S(1)} %fusion.35), channel_id=1, source_target_pairs={{0,24},{4,28},{8,0},{12,4},{16,8},{20,12},{24,16},{28,20},{1,25},{... | collective-permute-start | bytes 196616 | tf_op jit(solution)/shard_map/ppermute | solution.py:37
  64.3 4.5 %copy-start.4 = (f32[1,4,128,128]{3,2,1,0:T(8,128)S(1)}, f32[1,4,128,128]{3,2,1,0:T(8,128)}, u32[]{:S(2)}) copy-start(f32[1,4,128,128]{3,2,1,0:T(8,128)} %param.15) | copy-start | bytes 786436
  105.2 4.3 %copy-start.7 = (s32[4]{0:T(128)}, s32[4]{0:T(128)S(1)}, u32[]{:S(2)}) copy-start(s32[4]{0:T(128)S(1)} %get-tuple-element.988) | copy-start | bytes 52
  105.2 5.0 %collective-permute-start.6 = (f32[1,2,32,256]{3,2,1,0:T(8,128)S(1)}, f32[1,2,32,256]{3,2,1,0:T(8,128)S(1)}, u32[]{:S(2)}, u32[]{:S(2)}) collective-permute-start(f32[1,2,32,256]{3,2,1,0:T(8,128)S(1)} %get-tuple-element.546), channel_id=1, source_target_pairs={{0,24},{4,28},{8,0},{12,4},{16,8},{20,12},{24,16},{28,20},{1,25},{... | collective-permute-start | bytes 196616 | tf_op jit(solution)/shard_map/ppermute | solution.py:37
  106.8 3.5 %collective-permute-start.7 = (f32[1,2,32,256]{3,2,1,0:T(8,128)S(1)}, f32[1,2,32,256]{3,2,1,0:T(8,128)S(1)}, u32[]{:S(2)}, u32[]{:S(2)}) collective-permute-start(f32[1,2,32,256]{3,2,1,0:T(8,128)S(1)} %get-tuple-element.549), channel_id=1, source_target_pairs={{0,28},{4,0},{8,4},{12,8},{16,12},{20,16},{24,20},{28,24},{1,29},{... | collective-permute-start | bytes 196616 | tf_op jit(solution)/shard_map/ppermute | solution.py:37
  108.1 4.7 %collective-permute-start.8 = (f32[1,2,32,256]{3,2,1,0:T(8,128)S(1)}, f32[1,2,32,256]{3,2,1,0:T(8,128)S(1)}, u32[]{:S(2)}, u32[]{:S(2)}) collective-permute-start(f32[1,2,32,256]{3,2,1,0:T(8,128)S(1)} %get-tuple-element.548), channel_id=1, source_target_pairs={{0,4},{4,8},{8,12},{12,16},{16,20},{20,24},{24,28},{28,0},{1,5},{5... | collective-permute-start | bytes 196616 | tf_op jit(solution)/shard_map/ppermute | solution.py:37
  108.1 6.7 %collective-permute-start.9 = (f32[1,2,32,256]{3,2,1,0:T(8,128)S(1)}, f32[1,2,32,256]{3,2,1,0:T(8,128)S(1)}, u32[]{:S(2)}, u32[]{:S(2)}) collective-permute-start(f32[1,2,32,256]{3,2,1,0:T(8,128)S(1)} %get-tuple-element.547), channel_id=1, source_target_pairs={{0,8},{4,12},{8,16},{12,20},{16,24},{20,28},{24,0},{28,4},{1,9},{5... | collective-permute-start | bytes 196616 | tf_op jit(solution)/shard_map/ppermute | solution.py:37
  114.8 5.4 %collective-permute-start.14 = (f32[1,2,32,256]{3,2,1,0:T(8,128)S(1)}, f32[1,2,32,256]{3,2,1,0:T(8,128)S(1)}, u32[]{:S(2)}, u32[]{:S(2)}) collective-permute-start(f32[1,2,32,256]{3,2,1,0:T(8,128)S(1)} %add_divide_fusion.1), channel_id=1, source_target_pairs={{0,8},{4,12},{8,16},{12,20},{16,24},{20,28},{24,0},{28,4},{1,9},{5... | collective-permute-start | bytes 196616 | tf_op jit(solution)/shard_map/ppermute | solution.py:37
  114.9 5.4 %collective-permute-start.15 = (f32[1,2,32,256]{3,2,1,0:T(8,128)S(1)}, f32[1,2,32,256]{3,2,1,0:T(8,128)S(1)}, u32[]{:S(2)}, u32[]{:S(2)}) collective-permute-start(f32[1,2,32,256]{3,2,1,0:T(8,128)S(1)} %add_divide_fusion.1), channel_id=1, source_target_pairs={{0,4},{4,8},{8,12},{12,16},{16,20},{20,24},{24,28},{28,0},{1,5},{5... | collective-permute-start | bytes 196616 | tf_op jit(solution)/shard_map/ppermute | solution.py:37
  114.9 5.3 %collective-permute-start.16 = (f32[1,2,32,256]{3,2,1,0:T(8,128)S(1)}, f32[1,2,32,256]{3,2,1,0:T(8,128)S(1)}, u32[]{:S(2)}, u32[]{:S(2)}) collective-permute-start(f32[1,2,32,256]{3,2,1,0:T(8,128)S(1)} %add_divide_fusion.1), channel_id=1, source_target_pairs={{0,28},{4,0},{8,4},{12,8},{16,12},{20,16},{24,20},{28,24},{1,29},{... | collective-permute-start | bytes 196616 | tf_op jit(solution)/shard_map/ppermute | solution.py:37
  117.6 4.5 %collective-permute-start.17 = (f32[1,2,32,256]{3,2,1,0:T(8,128)S(1)}, f32[1,2,32,256]{3,2,1,0:T(8,128)S(1)}, u32[]{:S(2)}, u32[]{:S(2)}) collective-permute-start(f32[1,2,32,256]{3,2,1,0:T(8,128)S(1)} %add_divide_fusion.1), channel_id=1, source_target_pairs={{0,24},{4,28},{8,0},{12,4},{16,8},{20,12},{24,16},{28,20},{1,25},{... | collective-permute-start | bytes 196616 | tf_op jit(solution)/shard_map/ppermute | solution.py:37
  130.7 4.5 %copy-start.5 = (f32[1,4,128,128]{3,2,1,0:T(8,128)S(1)}, f32[1,4,128,128]{3,2,1,0:T(8,128)}, u32[]{:S(2)}) copy-start(f32[1,4,128,128]{3,2,1,0:T(8,128)} %param.15) | copy-start | bytes 786436
  139.7 2.5 copy-start.8
  171.3 4.9 %collective-permute-start.18 = (f32[1,2,32,256]{3,2,1,0:T(8,128)S(1)}, f32[1,2,32,256]{3,2,1,0:T(8,128)S(1)}, u32[]{:S(2)}, u32[]{:S(2)}) collective-permute-start(f32[1,2,32,256]{3,2,1,0:T(8,128)S(1)} %get-tuple-element.542), channel_id=1, source_target_pairs={{0,24},{4,28},{8,0},{12,4},{16,8},{20,12},{24,16},{28,20},{1,25},{... | collective-permute-start | bytes 196616 | tf_op jit(solution)/shard_map/ppermute | solution.py:37
  173.9 3.6 %collective-permute-start.19 = (f32[1,2,32,256]{3,2,1,0:T(8,128)S(1)}, f32[1,2,32,256]{3,2,1,0:T(8,128)S(1)}, u32[]{:S(2)}, u32[]{:S(2)}) collective-permute-start(f32[1,2,32,256]{3,2,1,0:T(8,128)S(1)} %get-tuple-element.545), channel_id=1, source_target_pairs={{0,28},{4,0},{8,4},{12,8},{16,12},{20,16},{24,20},{28,24},{1,29},{... | collective-permute-start | bytes 196616 | tf_op jit(solution)/shard_map/ppermute | solution.py:37
  173.9 4.6 %collective-permute-start.20 = (f32[1,2,32,256]{3,2,1,0:T(8,128)S(1)}, f32[1,2,32,256]{3,2,1,0:T(8,128)S(1)}, u32[]{:S(2)}, u32[]{:S(2)}) collective-permute-start(f32[1,2,32,256]{3,2,1,0:T(8,128)S(1)} %get-tuple-element.544), channel_id=1, source_target_pairs={{0,4},{4,8},{8,12},{12,16},{16,20},{20,24},{24,28},{28,0},{1,5},{5... | collective-permute-start | bytes 196616 | tf_op jit(solution)/shard_map/ppermute | solution.py:37
  174.4 5.5 %collective-permute-start.21 = (f32[1,2,32,256]{3,2,1,0:T(8,128)S(1)}, f32[1,2,32,256]{3,2,1,0:T(8,128)S(1)}, u32[]{:S(2)}, u32[]{:S(2)}) collective-permute-start(f32[1,2,32,256]{3,2,1,0:T(8,128)S(1)} %get-tuple-element.543), channel_id=1, source_target_pairs={{0,8},{4,12},{8,16},{12,20},{16,24},{20,28},{24,0},{28,4},{1,9},{5... | collective-permute-start | bytes 196616 | tf_op jit(solution)/shard_map/ppermute | solution.py:37
  180.0 5.6 %collective-permute-start.22 = (f32[1,2,32,256]{3,2,1,0:T(8,128)S(1)}, f32[1,2,32,256]{3,2,1,0:T(8,128)S(1)}, u32[]{:S(2)}, u32[]{:S(2)}) collective-permute-start(f32[1,2,32,256]{3,2,1,0:T(8,128)S(1)} %add_divide_fusion), channel_id=1, source_target_pairs={{0,8},{4,12},{8,16},{12,20},{16,24},{20,28},{24,0},{28,4},{1,9},{5... | collective-permute-start | bytes 196616 | tf_op jit(solution)/shard_map/ppermute | solution.py:37
  180.9 5.0 %collective-permute-start.23 = (f32[1,2,32,256]{3,2,1,0:T(8,128)S(1)}, f32[1,2,32,256]{3,2,1,0:T(8,128)S(1)}, u32[]{:S(2)}, u32[]{:S(2)}) collective-permute-start(f32[1,2,32,256]{3,2,1,0:T(8,128)S(1)} %add_divide_fusion), channel_id=1, source_target_pairs={{0,4},{4,8},{8,12},{12,16},{16,20},{20,24},{24,28},{28,0},{1,5},{5... | collective-permute-start | bytes 196616 | tf_op jit(solution)/shard_map/ppermute | solution.py:37
  180.9 5.0 %collective-permute-start.24 = (f32[1,2,32,256]{3,2,1,0:T(8,128)S(1)}, f32[1,2,32,256]{3,2,1,0:T(8,128)S(1)}, u32[]{:S(2)}, u32[]{:S(2)}) collective-permute-start(f32[1,2,32,256]{3,2,1,0:T(8,128)S(1)} %add_divide_fusion), channel_id=1, source_target_pairs={{0,28},{4,0},{8,4},{12,8},{16,12},{20,16},{24,20},{28,24},{1,29},{... | collective-permute-start | bytes 196616 | tf_op jit(solution)/shard_map/ppermute | solution.py:37
  183.6 4.3 %collective-permute-start.25 = (f32[1,2,32,256]{3,2,1,0:T(8,128)S(1)}, f32[1,2,32,256]{3,2,1,0:T(8,128)S(1)}, u32[]{:S(2)}, u32[]{:S(2)}) collective-permute-start(f32[1,2,32,256]{3,2,1,0:T(8,128)S(1)} %add_divide_fusion), channel_id=1, source_target_pairs={{0,24},{4,28},{8,0},{12,4},{16,8},{20,12},{24,16},{28,20},{1,25},{... | collective-permute-start | bytes 196616 | tf_op jit(solution)/shard_map/ppermute | solution.py:37
  196.9 4.5 %copy-start.6 = (f32[1,4,128,128]{3,2,1,0:T(8,128)S(1)}, f32[1,4,128,128]{3,2,1,0:T(8,128)}, u32[]{:S(2)}) copy-start(f32[1,4,128,128]{3,2,1,0:T(8,128)} %param.15) | copy-start | bytes 786436
  237.5 4.3 %collective-permute-start.26 = (f32[1,2,32,256]{3,2,1,0:T(8,128)S(1)}, f32[1,2,32,256]{3,2,1,0:T(8,128)S(1)}, u32[]{:S(2)}, u32[]{:S(2)}) collective-permute-start(f32[1,2,32,256]{3,2,1,0:T(8,128)S(1)} %get-tuple-element.538), channel_id=1, source_target_pairs={{0,24},{4,28},{8,0},{12,4},{16,8},{20,12},{24,16},{28,20},{1,25},{... | collective-permute-start | bytes 196616 | tf_op jit(solution)/shard_map/ppermute | solution.py:37
  239.5 3.6 %collective-permute-start.27 = (f32[1,2,32,256]{3,2,1,0:T(8,128)S(1)}, f32[1,2,32,256]{3,2,1,0:T(8,128)S(1)}, u32[]{:S(2)}, u32[]{:S(2)}) collective-permute-start(f32[1,2,32,256]{3,2,1,0:T(8,128)S(1)} %get-tuple-element.541), channel_id=1, source_target_pairs={{0,28},{4,0},{8,4},{12,8},{16,12},{20,16},{24,20},{28,24},{1,29},{... | collective-permute-start | bytes 196616 | tf_op jit(solution)/shard_map/ppermute | solution.py:37
  239.5 4.6 %collective-permute-start.28 = (f32[1,2,32,256]{3,2,1,0:T(8,128)S(1)}, f32[1,2,32,256]{3,2,1,0:T(8,128)S(1)}, u32[]{:S(2)}, u32[]{:S(2)}) collective-permute-start(f32[1,2,32,256]{3,2,1,0:T(8,128)S(1)} %get-tuple-element.540), channel_id=1, source_target_pairs={{0,4},{4,8},{8,12},{12,16},{16,20},{20,24},{24,28},{28,0},{1,5},{5... | collective-permute-start | bytes 196616 | tf_op jit(solution)/shard_map/ppermute | solution.py:37
  240.0 5.5 %collective-permute-start.29 = (f32[1,2,32,256]{3,2,1,0:T(8,128)S(1)}, f32[1,2,32,256]{3,2,1,0:T(8,128)S(1)}, u32[]{:S(2)}, u32[]{:S(2)}) collective-permute-start(f32[1,2,32,256]{3,2,1,0:T(8,128)S(1)} %get-tuple-element.539), channel_id=1, source_target_pairs={{0,8},{4,12},{8,16},{12,20},{16,24},{20,28},{24,0},{28,4},{1,9},{5... | collective-permute-start | bytes 196616 | tf_op jit(solution)/shard_map/ppermute | solution.py:37
  245.6 4.1 %collective-permute-start.30 = (f32[1,2,8,256]{3,2,1,0:T(8,128)S(1)}, f32[1,2,8,256]{3,2,1,0:T(8,128)S(1)}, u32[]{:S(2)}, u32[]{:S(2)}) collective-permute-start(f32[1,2,8,256]{3,2,1,0:T(8,128)S(1)} %get-tuple-element.556), channel_id=1, source_target_pairs={{0,4},{4,8},{8,12},{12,16},{16,20},{20,24},{24,28},{28,0},{1,5},{5... | collective-permute-start | bytes 49160 | tf_op jit(solution)/shard_map/ppermute | solution.py:26
  245.6 4.1 %collective-permute-start.31 = (f32[1,2,8,256]{3,2,1,0:T(8,128)S(1)}, f32[1,2,8,256]{3,2,1,0:T(8,128)S(1)}, u32[]{:S(2)}, u32[]{:S(2)}) collective-permute-start(f32[1,2,8,256]{3,2,1,0:T(8,128)S(1)} %get-tuple-element.557), channel_id=1, source_target_pairs={{4,0},{8,4},{12,8},{16,12},{20,16},{24,20},{28,24},{0,28},{5,1},{9... | collective-permute-start | bytes 49160 | tf_op jit(solution)/shard_map/ppermute | solution.py:29
where the time goes:
time: 273 us; the launch traced here: 269 us
  local copies, waits for them, and re-layouts  73.6 us (27%)
  loops' own time  65.7 us (24%)
  matrix products  42.5 us (16%)
  waiting for transfers between devices  35.6 us (13%)
  starting transfers between devices  31.1 us (11%)
  blocking collectives  15.3 us (6%)
  other arithmetic  4.05 us (1%)
    another operation x4, loops' own time, deposit(): return lax.fori_loop(0, frame_total, add_one, target)  65.2 us
    ppermute x28, waiting for transfers between devices, passed_along(): return lax.ppermute(value, axis, pairs)  34.2 us
    dynamic_update_slice x16, local copies, waits for them, and re-layouts, add_one(): return lax.dynamic_update_slice(running, current + addition, corner)  25.4 us
    ppermute x28, starting transfers between devices, passed_along(): return lax.ppermute(value, axis, pairs)  25 us
    gather x36, local copies, waits for them, and re-layouts  23.8 us
    dynamic_slice x32, local copies, waits for them, and re-layouts, add_one(): corner = (0,) * leading + (start_cols[frame_index], start_rows[frame_index])  20.8 us
    all_gather x1, blocking collectives, per_device(): every_rim = lax.all_gather(change_rim, 'ang', axis=0, tiled=True)  15.3 us
    ppermute x2, starting transfers between devices, padded_2(): lax.ppermute(lax.slice_in_dim(block, 0, width, axis=dim), axis, backward)  5.5 us
  transfers between devices with their start and end apart: 32, of which 20 were waited for; matrix products, arithmetic and copies ran while one was open for 18% of the time, Pallas kernels for 0%

commit v1 on v0

v1 whole, which is shorter than its diff:
```python
import functools

import jax
import jax.numpy as jnp
import numpy as np
from jax import lax
from jax.experimental import pallas as pl
from jax.experimental.pallas import tpu as pltpu
from jax.sharding import PartitionSpec as P

SH = 8
ITERS = 3
MODULUS_FLOOR = 0.25
INTERSECTION_WEIGHT = 1.0
RELAXATION = 0.5
MESH = pl.DeviceIdType.MESH
F32 = jnp.float32
BF16 = jnp.bfloat16


def dft_tables(length):
    index = np.arange(length)
    phases = (index[:, None] * index[None, :] % length) * (2.0 * np.pi / length)
    cosine = np.cos(phases) / np.sqrt(length)
    sine = np.sin(phases) / np.sqrt(length)
    a = np.block([[cosine, sine], [-sine, cosine]])
    parts = []
    for table in (a, a.T):
        high = table.astype(np.float32).astype(jnp.bfloat16)
        low = (table - high.astype(np.float64)).astype(np.float32).astype(jnp.bfloat16)
        parts += [high, low]
    return np.stack(parts)


def split(x):
    high = x.astype(BF16)
    return high, (x - high.astype(F32)).astype(BF16)


def dot(a, b):
    return jnp.dot(a, b, preferred_element_type=F32)


def times_right(x, high, low):
    x_high, x_low = split(x)
    return dot(x_high, high) + (dot(x_low, high) + dot(x_high, low))


def times_left(high, low, x):
    x_high, x_low = split(x)
    return dot(high, x_high) + (dot(high, x_low) + dot(low, x_high))


def update_kernel(
    n_pos, n_ang,
    positions, steps, object_hbm, probe, intensity, tables,
    gathered,
    held, rolled, amplitude, cover, cover_in, inverse, canvas, rim_in, first, source, summed, sums_in,
    load_sem, cover_send, cover_recv, rim_send, rim_recv, est_send, est_recv,
    sum_send, sum_recv, edge_send, edge_recv, core_send, core_recv, side_send, side_recv,
):
    me = lax.axis_index("pos")
    ang = lax.axis_index("ang")
    layers, tile, rows = held.shape[1], first.shape[1], first.shape[2]
    frame = probe.shape[1]
    half = rows - frame
    frames = positions.shape[0]
    bands = source.shape[1] // tile
    reach = bands // 2
    width = n_pos * tile
    offsets = [t for t in range(bands) if t != reach]

    def at(shift):
        return lax.rem(me + (shift + n_pos), n_pos)

    def peer(shift):
        return lax.rem(ang + (shift + n_ang), n_ang)

    load = pltpu.make_async_copy(object_hbm, held, load_sem)
    load.start()

    barrier = pltpu.get_barrier_semaphore()
    for t in offsets:
        pl.semaphore_signal(barrier, inc=1, device_id={"pos": at(t - reach)}, device_id_type=MESH)
    for d in range(1, n_ang):
        pl.semaphore_signal(barrier, inc=1, device_id={"ang": peer(d)}, device_id_type=MESH)

    lane = lax.broadcasted_iota(jnp.int32, (tile, frame), 1)
    row = lax.broadcasted_iota(jnp.int32, (tile, frame), 0)
    col_at = []
    row_at = []
    for j in range(frames):
        col_at.append(lax.rem(positions[j, 0] - me * tile + (reach * tile + width), width))
        row_at.append(positions[j, 1])

    def unfold(j, block, target, channel, is_first):
        low_half = lane >= row_at[j]
        low_cols = row >= col_at[j]
        zero = jnp.zeros((tile, frame), F32)

        def put(at_row, at_lane, value):
            index = (pl.ds(at_row, tile), pl.ds(at_lane, frame))
            index = index if channel is None else (channel,) + index
            if is_first:
                target[index] = value
            else:
                target[index] += value

        for t in range(bands - 1):
            piece = block[t * tile : (t + 1) * tile]
            low = jnp.where(low_half, piece, zero)
            high = jnp.where(low_half, zero, piece)
            if t == 0:
                put(0, 0, jnp.where(low_cols, low, zero))
                put(0, half, jnp.where(low_cols, high, zero))
                put((bands - 1) * tile, 0, jnp.where(low_cols, zero, low))
                put((bands - 1) * tile, half, jnp.where(low_cols, zero, high))
            else:
                put(t * tile, 0, low)
                put(t * tile, half, high)

    for j in range(frames):
        power = None
        for channel in range(2):
            value = pltpu.roll(probe[channel], col_at[j], 0)
            value = pltpu.roll(value, lax.rem(row_at[j], frame), 1)
            rolled[j, channel] = value
            power = value * value if power is None else power + value * value
        unfold(j, power, cover, None, j == 0)
        amplitude[j] = jnp.sqrt(intensity[j])

    pl.semaphore_wait(barrier, len(offsets) + n_ang - 1)

    def cover_copy(t):
        return pltpu.make_async_remote_copy(
            src_ref=cover.at[pl.ds(t * tile, tile), :], dst_ref=cover_in.at[t],
            send_sem=cover_send.at[t], recv_sem=cover_recv.at[t],
            device_id={"pos": at(t - reach)}, device_id_type=MESH)

    for t in offsets:
        cover_copy(t).start()

    wide = tile + 2 * SH
    per_block = frame // tile
    lane_wide = lax.broadcasted_iota(jnp.int32, (wide, frame), 1)
    source_col = lax.rem(lane_wide, tile)
    layer_in = lane_wide // tile
    target_col = lax.broadcasted_iota(jnp.int32, (wide, frame), 0) - SH
    blocks = []
    for begin in range(0, layers, per_block):
        shift = jnp.full((wide, frame), steps[ang, begin], jnp.int32)
        for k in range(1, per_block):
            shift = jnp.where(layer_in == k, steps[ang, begin + k], shift)
        blocks.append(jnp.where(source_col == target_col + shift, 1.0, 0.0).astype(BF16))
    pick = jnp.concatenate(blocks, axis=1)
    load.wait()
    for channel in range(2):
        high, low = split(held[channel].reshape(layers * tile, rows))
        canvas[channel] = dot(pick, high) + dot(pick, low)

    def rim_copy(side):
        begin = 0 if side == 0 else SH + tile
        return pltpu.make_async_remote_copy(
            src_ref=canvas.at[:, pl.ds(begin, SH), :], dst_ref=rim_in.at[side],
            send_sem=rim_send.at[side], recv_sem=rim_recv.at[side],
            device_id={"pos": at(-1 if side == 0 else 1)}, device_id_type=MESH)

    for side in range(2):
        rim_copy(side).start()
    mine = pl.ds(reach * tile, tile)
    for side in range(2):
        rim_copy(side).wait()
    for channel in range(2):
        low = canvas[channel, pl.ds(SH, SH), :] + rim_in[1, channel]
        middle = canvas[channel, pl.ds(2 * SH, tile - 2 * SH), :]
        high = canvas[channel, pl.ds(tile, SH), :] + rim_in[0, channel]
        value = jnp.concatenate([low, middle, high], axis=0)
        first[channel] = value
        source[channel, mine, :] = value

    def est_copy(t):
        return pltpu.make_async_remote_copy(
            src_ref=source.at[:, mine, :], dst_ref=source.at[:, pl.ds(t * tile, tile), :],
            send_sem=est_send.at[t], recv_sem=est_recv.at[t],
            device_id={"pos": at(reach - t)}, device_id_type=MESH)

    def sum_copy(t):
        return pltpu.make_async_remote_copy(
            src_ref=summed.at[:, pl.ds(t * tile, tile), :], dst_ref=sums_in.at[t],
            send_sem=sum_send.at[t], recv_sem=sum_recv.at[t],
            device_id={"pos": at(t - reach)}, device_id_type=MESH)

    def patch(j, channel):
        low_half = lane >= row_at[j]
        low_cols = row >= col_at[j]
        pieces = []
        for t in range(bands):
            cols = pl.ds(t * tile, tile)
            pieces.append(jnp.where(
                low_half, source[channel, cols, pl.ds(0, frame)], source[channel, cols, pl.ds(half, frame)]))
        pieces[0] = jnp.where(low_cols, pieces[0], pieces[-1])
        return jnp.concatenate(pieces[:-1], axis=0)

    def transform_pair(pair):
        a_high, a_low, b_high, b_low = tables[0], tables[1], tables[2], tables[3]
        stacked = []
        for j in pair:
            real, imag = patch(j, 0), patch(j, 1)
            p_real, p_imag = rolled[j, 0], rolled[j, 1]
            stacked.append(jnp.concatenate(
                [p_real * real - p_imag * imag, p_real * imag + p_imag * real], axis=1))
        out = times_right(jnp.concatenate(stacked, axis=0), b_high, b_low)
        columns = []
        for k in range(len(pair)):
            block = out[k * frame : (k + 1) * frame]
            columns.append(jnp.concatenate([block[:, :frame], block[:, frame:]], axis=0))
        wave = times_left(a_high, a_low, jnp.concatenate(columns, axis=1))
        real, imag = wave[:frame], wave[frame:]
        amp = jnp.concatenate([amplitude[j] for j in pair], axis=1)
        factor = amp * jnp.minimum(lax.rsqrt(real * real + imag * imag), 1.0 / MODULUS_FLOOR)
        back = times_left(b_high, b_low, jnp.concatenate([real * factor, imag * factor], axis=0))
        stacked = []
        for k in range(len(pair)):
            block = back[:, k * frame : (k + 1) * frame]
            stacked.append(jnp.concatenate([block[:frame], block[frame:]], axis=1))
        return times_right(jnp.concatenate(stacked, axis=0), a_high, a_low)

    def iterate(iteration, carry):
        for t in offsets:
            est_copy(t).start()

        @pl.when(iteration == 0)
        def _():
            for t in offsets:
                cover_copy(t).wait()
            total = cover[mine, :]
            for t in offsets:
                total = total + cover_in[t]
            inverse[...] = 1.0 / (total + INTERSECTION_WEIGHT)

        for t in offsets:
            est_copy(t).wait()
        step = 2 if frames % 2 == 0 else 1
        for begin in range(0, frames, step):
            pair = list(range(begin, begin + step))
            out = transform_pair(pair)
            for k, j in enumerate(pair):
                block = out[k * frame : (k + 1) * frame]
                real, imag = block[:, :frame], block[:, frame:]
                p_real, p_imag = rolled[j, 0], rolled[j, 1]
                unfold(j, p_real * real + p_imag * imag, summed, 0, j == 0)
                unfold(j, p_real * imag - p_imag * real, summed, 1, j == 0)
        for t in offsets:
            sum_copy(t).start()
        for t in offsets:
            sum_copy(t).wait()
        for channel in range(2):
            total = summed[channel, mine, :]
            for t in offsets:
                total = total + sums_in[t, channel]
            old = source[channel, mine, :]
            source[channel, mine, :] = (total + INTERSECTION_WEIGHT * old) * inverse[...]
        return carry

    lax.fori_loop(0, ITERS, iterate, 0)

    for channel in range(2):
        gathered[ang, channel, pl.ds(SH, tile), :] = source[channel, mine, :] - first[channel]

    def edge_copy(side):
        begin, end = (SH, SH + tile) if side == 0 else (tile, 0)
        return pltpu.make_async_remote_copy(
            src_ref=gathered.at[ang, :, pl.ds(begin, SH), :], dst_ref=gathered.at[ang, :, pl.ds(end, SH), :],
            send_sem=edge_send.at[side], recv_sem=edge_recv.at[side],
            device_id={"pos": at(-1 if side == 0 else 1)}, device_id_type=MESH)

    def core_copy(d, slot):
        part = gathered.at[slot, :, pl.ds(SH, tile), :]
        return pltpu.make_async_remote_copy(
            src_ref=part, dst_ref=part, send_sem=core_send.at[d], recv_sem=core_recv.at[d],
            device_id={"ang": peer(d)}, device_id_type=MESH)

    def side_copy(d, side, slot):
        part = gathered.at[slot, :, pl.ds(0 if side == 0 else SH + tile, SH), :]
        return pltpu.make_async_remote_copy(
            src_ref=part, dst_ref=part, send_sem=side_send.at[d, side], recv_sem=side_recv.at[d, side],
            device_id={"ang": peer(d)}, device_id_type=MESH)

    for side in range(2):
        edge_copy(side).start()
    for d in range(1, n_ang):
        core_copy(d, ang).start()
    for side in range(2):
        edge_copy(side).wait()
    for d in range(1, n_ang):
        for side in range(2):
            side_copy(d, side, ang).start()
    for d in range(1, n_ang):
        core_copy(d, ang).wait_send()
        core_copy(d, peer(-d)).wait_recv()
        for side in range(2):
            side_copy(d, side, ang).wait_send()
            side_copy(d, side, peer(-d)).wait_recv()


def spread_kernel(weight, steps, object_block, gathered, out):
    _, depth, tile, rows = object_block.shape
    n_ang, _, wide, _ = gathered.shape
    first_layer = pl.program_id(0) * depth
    lane = lax.broadcasted_iota(jnp.int32, (tile, n_ang * wide), 1)
    offset = lane - lax.broadcasted_iota(jnp.int32, (tile, n_ang * wide), 0)
    blocks = []
    for z in range(depth):
        chosen = None
        for a in range(n_ang):
            begin = a * wide
            inside = (lane >= begin) & (lane < begin + wide)
            hit = inside & (offset == begin + SH - steps[a, first_layer + z])
            chosen = hit if chosen is None else chosen | hit
        blocks.append(jnp.where(chosen, 1.0, 0.0))
    pick = jnp.concatenate(blocks, axis=0).astype(BF16)
    for channel in range(2):
        high, low = split(gathered[:, channel].reshape(n_ang * wide, rows))
        total = dot(pick, high) + dot(pick, low)
        out[channel] = object_block[channel] + weight * total.reshape(depth, tile, rows)


def per_device(n_pos, n_ang, object_field, probe_wave, intensity, positions, shear_steps):
    _, layers, tile, rows = object_field.shape
    frame = probe_wave.shape[1]
    frames = positions.shape[0]
    reach = -(-(frame // 2) // tile)
    bands = 2 * reach + 1
    assert intensity.shape[0] == 1 and frame == 2 * reach * tile and rows == 2 * frame
    assert n_pos >= bands
    tables = jnp.asarray(dft_tables(frame))
    wide = tile + 2 * SH
    vmem = pl.BlockSpec(memory_space=pltpu.VMEM)
    smem = pl.BlockSpec(memory_space=pltpu.SMEM)
    dma = pltpu.SemaphoreType.DMA
    gathered = pl.pallas_call(
        functools.partial(update_kernel, n_pos, n_ang),
        out_shape=jax.ShapeDtypeStruct((n_ang, 2, wide, rows), F32),
        in_specs=[smem, smem, pl.BlockSpec(memory_space=pl.ANY), vmem, vmem, vmem],
        out_specs=vmem,
        scratch_shapes=[
            pltpu.VMEM((2, layers, tile, rows), F32),
            pltpu.VMEM((frames, 2, frame, frame), F32),
            pltpu.VMEM((frames, frame, frame), F32),
            pltpu.VMEM((bands * tile, rows), F32),
            pltpu.VMEM((bands, tile, rows), F32),
            pltpu.VMEM((tile, rows), F32),
            pltpu.VMEM((2, wide, rows), F32),
            pltpu.VMEM((2, 2, SH, rows), F32),
            pltpu.VMEM((2, tile, rows), F32),
            pltpu.VMEM((2, bands * tile, rows), F32),
            pltpu.VMEM((2, bands * tile, rows), F32),
            pltpu.VMEM((bands, 2, tile, rows), F32),
            dma,
            dma((bands,)), dma((bands,)), dma((2,)), dma((2,)), dma((bands,)), dma((bands,)),
            dma((bands,)), dma((bands,)), dma((2,)), dma((2,)), dma((n_ang,)), dma((n_ang,)),
            dma((n_ang, 2)), dma((n_ang, 2)),
        ],
        compiler_params=pltpu.CompilerParams(collective_id=0, has_side_effects=True),
        name="update",
    )(positions, shear_steps, object_field, probe_wave, intensity[0], tables)

    depth = 8 if layers % 8 == 0 else layers
    block = pl.BlockSpec((2, depth, tile, rows), lambda i: (0, i, 0, 0))
    return pl.pallas_call(
        functools.partial(spread_kernel, RELAXATION / shear_steps.shape[0]),
        out_shape=jax.ShapeDtypeStruct(object_field.shape, F32),
        grid=(layers // depth,),
        in_specs=[smem, block, vmem],
        out_specs=block,
        name="spread",
    )(shear_steps, object_field, gathered)


def solution(mesh):
    placed = (P(None, None, "pos", None), P(), P("ang", "pos", None, None), P("pos", None), P())
    return jax.shard_map(
        functools.partial(per_device, mesh.shape["pos"], mesh.shape["ang"]),
        mesh=mesh,
        in_specs=placed,
        out_specs=P(None, None, "pos", None),
        check_vma=False,
    )
```

time: 273 us -> 69.7 us (0.26); the launches traced: 269 us -> 69.5 us
  local copies, waits for them, and re-layouts: 73.6 us -> 1.34 us
  Pallas kernels: 0 us -> 68.2 us
  loops' own time: 65.7 us -> 0 us
  matrix products: 42.5 us -> 0 us
  waiting for transfers between devices: 35.6 us -> 0 us
  starting transfers between devices: 31.1 us -> 0 us
  blocking collectives: 15.3 us -> 0 us
  other arithmetic: 4.05 us -> 0 us
    pallas_call x0 -> x2, Pallas kernels: none -> 68.2 us  [the longest x1 63.5 us: per_device(): pl.pallas_call(functools.partial(update_kernel, n_pos, n_ang), out_shape=...]
    another operation x7 -> x0, loops' own time: 65.7 us -> none  [the longest x4 65.2 us: deposit(): return lax.fori_loop(0, frame_total, add_one, target)]
    dot_general x50 -> x0, matrix products: 42.5 us -> none  [the longest x6 5.18 us: transform(): jnp.einsum('abjk,kl->abjl', left_imag, sine_table, precision=HIGHEST)]
    ppermute x32 -> x0, waiting for transfers between devices: 35.6 us -> none  [the longest x28 34.2 us: passed_along(): return lax.ppermute(value, axis, pairs)]
    ppermute x32 -> x0, starting transfers between devices: 31.1 us -> none  [the longest x28 25 us: passed_along(): return lax.ppermute(value, axis, pairs)]
    dynamic_update_slice x16 -> x0, local copies, waits for them, and re-layouts: 25.4 us -> none  [add_one(): return lax.dynamic_update_slice(running, current + addition, corner)]
    gather x36 -> x0, local copies, waits for them, and re-layouts: 23.8 us -> none
    dynamic_slice x32 -> x0, local copies, waits for them, and re-layouts: 20.8 us -> none  [add_one(): corner = (0,) * leading + (start_cols[frame_index], start_rows[frame_index])]
  transfers between devices with their start and end apart: 32 -> 0, of which waited for: 20 -> 0; matrix products, arithmetic and copies ran while one was open for 18% -> 0% of each run, Pallas kernels for 0% -> 0%
where the time goes in v1:
time: 69.7 us; the launch traced here: 69.5 us
  Pallas kernels  68.2 us (98%)
  local copies, waits for them, and re-layouts  1.34 us (2%)
    pallas_call x1, Pallas kernels, per_device(): pl.pallas_call(functools.partial(update_kernel, n_pos, n_ang), out_shape=...  63.5 us
    pallas_call x1, Pallas kernels, per_device(): pl.pallas_call(functools.partial(spread_kernel, RELAXATION / shear_steps....  4.64 us

profile of v1, /device:TPU:0, one launch (start us, length us, event | category | flops | bytes accessed | tf_op | source)
XLA Modules:
  0.0 69.5 jit_solution(6229613493310886056)
XLA Ops:
  0.0 1.3 %copy.7.positions = s32[4,2]{1,0:T(4,128)} copy(s32[4,2]{0,1:T(2,128)} %param.9) | data formatting | bytes 64 | tf_op args[3]
  1.3 63.5 %update.1.gathered = f32[4,2,48,256]{3,2,1,0:T(8,128)} custom-call(s32[4,2]{1,0:T(4,128)} %copy.7.positions, s32[4,32]{1,0:T(4,128)} %steps.3, f32[2,32,32,256]{3,2,1,0:T(8,128)} %object_block.1, f32[2,128,128]{2,1,0:T(8,128)} %probe.1, f32[4,128,128]{2,1,0:T(8,128)} %bitcast.1, bf16[4,256,256]{2,1,0:T(8,128)(2,1)} %constant.2.clone.tables), custom_call_target="tpu_custom_call" | custom-call | tf_op jit(solution)/shard_map/update/pallas_call | solution.py:341
  64.9 4.6 %spread.1 = f32[2,32,32,256]{3,2,1,0:T(8,128)} custom-call(s32[4,32]{1,0:T(4,128)} %steps.3, f32[2,32,32,256]{3,2,1,0:T(8,128)} %object_block.1, f32[4,2,48,256]{3,2,1,0:T(8,128)} %update.1.gathered), custom_call_target="tpu_custom_call" | custom-call | tf_op jit(solution)/shard_map/spread/pallas_call | solution.py:370

commit v2 on v1

--- a/solution.py
+++ b/solution.py
@@ -55,7 +55,7 @@
     n_pos, n_ang,
     positions, steps, object_hbm, probe, intensity, tables,
     gathered,
-    held, rolled, amplitude, cover, cover_in, inverse, canvas, rim_in, first, source, summed, sums_in,
+    held, rolled, amplitude, cover, cover_in, inverse, canvas, rim_in, first, source, summed, sums_in, waves,
     load_sem, cover_send, cover_recv, rim_send, rim_recv, est_send, est_recv,
     sum_send, sum_recv, edge_send, edge_recv, core_send, core_recv, side_send, side_recv,
 ):
@@ -64,7 +64,7 @@
     layers, tile, rows = held.shape[1], first.shape[1], first.shape[2]
     frame = probe.shape[1]
     half = rows - frame
-    frames = positions.shape[0]
+    frames = positions.shape[1]
     bands = source.shape[1] // tile
     reach = bands // 2
     width = n_pos * tile
@@ -90,55 +90,25 @@
     col_at = []
     row_at = []
     for j in range(frames):
-        col_at.append(lax.rem(positions[j, 0] - me * tile + (reach * tile + width), width))
-        row_at.append(positions[j, 1])
-
-    def unfold(j, block, target, channel, is_first):
-        low_half = lane >= row_at[j]
-        low_cols = row >= col_at[j]
+        col_at.append(lax.rem(positions[0, j] - me * tile + (reach * tile + width), width))
+        row_at.append(positions[1, j])
+
+    def unfold(t, pieces):
+        sums = [[None, None], [None, None]] if t == 0 else [[None, None]]
         zero = jnp.zeros((tile, frame), F32)
-
-        def put(at_row, at_lane, value):
-            index = (pl.ds(at_row, tile), pl.ds(at_lane, frame))
-            index = index if channel is None else (channel,) + index
-            if is_first:
-                target[index] = value
-            else:
-                target[index] += value
-
-        for t in range(bands - 1):
-            piece = block[t * tile : (t + 1) * tile]
-            low = jnp.where(low_half, piece, zero)
-            high = jnp.where(low_half, zero, piece)
-            if t == 0:
-                put(0, 0, jnp.where(low_cols, low, zero))
-                put(0, half, jnp.where(low_cols, high, zero))
-                put((bands - 1) * tile, 0, jnp.where(low_cols, zero, low))
-                put((bands - 1) * tile, half, jnp.where(low_cols, zero, high))
-            else:
-                put(t * tile, 0, low)
-                put(t * tile, half, high)
-
-    for j in range(frames):
-        power = None
-        for channel in range(2):
-            value = pltpu.roll(probe[channel], col_at[j], 0)
-            value = pltpu.roll(value, lax.rem(row_at[j], frame), 1)
-            rolled[j, channel] = value
-            power = value * value if power is None else power + value * value
-        unfold(j, power, cover, None, j == 0)
-        amplitude[j] = jnp.sqrt(intensity[j])
-
-    pl.semaphore_wait(barrier, len(offsets) + n_ang - 1)
-
-    def cover_copy(t):
-        return pltpu.make_async_remote_copy(
-            src_ref=cover.at[pl.ds(t * tile, tile), :], dst_ref=cover_in.at[t],
-            send_sem=cover_send.at[t], recv_sem=cover_recv.at[t],
-            device_id={"pos": at(t - reach)}, device_id_type=MESH)
-
-    for t in offsets:
-        cover_copy(t).start()
+        for j, piece in enumerate(pieces):
+            low_half = lane >= row_at[j]
+            parts = [jnp.where(low_half, piece, zero), jnp.where(low_half, zero, piece)]
+            for lanes in range(2):
+                values = [parts[lanes]]
+                if t == 0:
+                    low_cols = row >= col_at[j]
+                    values = [jnp.where(low_cols, parts[lanes], zero), jnp.where(low_cols, zero, parts[lanes])]
+                for place, value in enumerate(values):
+                    old = sums[place][lanes]
+                    sums[place][lanes] = value if old is None else old + value
+        targets = [t, bands - 1] if t == 0 else [t]
+        return [(target, jnp.concatenate(sums[place], axis=1)) for place, target in enumerate(targets)]
 
     wide = tile + 2 * SH
     per_block = frame // tile
@@ -158,6 +128,8 @@
         high, low = split(held[channel].reshape(layers * tile, rows))
         canvas[channel] = dot(pick, high) + dot(pick, low)
 
+    pl.semaphore_wait(barrier, len(offsets) + n_ang - 1)
+
     def rim_copy(side):
         begin = 0 if side == 0 else SH + tile
         return pltpu.make_async_remote_copy(
@@ -167,6 +139,23 @@
 
     for side in range(2):
         rim_copy(side).start()
+    for j in range(frames):
+        for channel in range(2):
+            value = pltpu.roll(probe[channel], col_at[j], 0)
+            rolled[j, channel] = pltpu.roll(value, lax.rem(row_at[j], frame), 1)
+        amplitude[:, pl.ds(j * frame, frame)] = jnp.sqrt(intensity[j])
+    for t in range(bands - 1):
+        cols = pl.ds(t * tile, tile)
+        powers = [rolled[j, 0, cols, :] ** 2 + rolled[j, 1, cols, :] ** 2 for j in range(frames)]
+        for target, value in unfold(t, powers):
+            cover[pl.ds(target * tile, tile), :] = value
+
+    def cover_copy(t):
+        return pltpu.make_async_remote_copy(
+            src_ref=cover.at[pl.ds(t * tile, tile), :], dst_ref=cover_in.at[t],
+            send_sem=cover_send.at[t], recv_sem=cover_recv.at[t],
+            device_id={"pos": at(t - reach)}, device_id_type=MESH)
+
     mine = pl.ds(reach * tile, tile)
     for side in range(2):
         rim_copy(side).wait()
@@ -190,44 +179,89 @@
             send_sem=sum_send.at[t], recv_sem=sum_recv.at[t],
             device_id={"pos": at(t - reach)}, device_id_type=MESH)
 
-    def patch(j, channel):
+    def fold(t, channel, j):
         low_half = lane >= row_at[j]
-        low_cols = row >= col_at[j]
-        pieces = []
-        for t in range(bands):
-            cols = pl.ds(t * tile, tile)
-            pieces.append(jnp.where(
-                low_half, source[channel, cols, pl.ds(0, frame)], source[channel, cols, pl.ds(half, frame)]))
-        pieces[0] = jnp.where(low_cols, pieces[0], pieces[-1])
-        return jnp.concatenate(pieces[:-1], axis=0)
-
-    def transform_pair(pair):
-        a_high, a_low, b_high, b_low = tables[0], tables[1], tables[2], tables[3]
+
+        def columns(at_tile):
+            cols = pl.ds(at_tile * tile, tile)
+            return jnp.where(
+                low_half, source[channel, cols, pl.ds(0, frame)], source[channel, cols, pl.ds(half, frame)])
+
+        if t > 0:
+            return columns(t)
+        return jnp.where(row >= col_at[j], columns(0), columns(bands - 1))
+
+    def forward_rows(t):
+        cols = pl.ds(t * tile, tile)
         stacked = []
-        for j in pair:
-            real, imag = patch(j, 0), patch(j, 1)
-            p_real, p_imag = rolled[j, 0], rolled[j, 1]
+        for j in range(frames):
+            real, imag = fold(t, 0, j), fold(t, 1, j)
+            p_real, p_imag = rolled[j, 0, cols, :], rolled[j, 1, cols, :]
             stacked.append(jnp.concatenate(
                 [p_real * real - p_imag * imag, p_real * imag + p_imag * real], axis=1))
-        out = times_right(jnp.concatenate(stacked, axis=0), b_high, b_low)
-        columns = []
-        for k in range(len(pair)):
-            block = out[k * frame : (k + 1) * frame]
-            columns.append(jnp.concatenate([block[:, :frame], block[:, frame:]], axis=0))
-        wave = times_left(a_high, a_low, jnp.concatenate(columns, axis=1))
+        out = times_right(jnp.concatenate(stacked, axis=0), tables[2], tables[3])
+        for j in range(frames):
+            block = out[j * tile : (j + 1) * tile]
+            lanes = pl.ds(j * frame, frame)
+            waves[cols, lanes] = block[:, :frame]
+            waves[pl.ds(frame + t * tile, tile), lanes] = block[:, frame:]
+
+    def correct(begin, count):
+        lanes = pl.ds(begin * frame, count * frame)
+        wave = times_left(tables[0], tables[1], waves[:, lanes])
         real, imag = wave[:frame], wave[frame:]
-        amp = jnp.concatenate([amplitude[j] for j in pair], axis=1)
-        factor = amp * jnp.minimum(lax.rsqrt(real * real + imag * imag), 1.0 / MODULUS_FLOOR)
-        back = times_left(b_high, b_low, jnp.concatenate([real * factor, imag * factor], axis=0))
+        factor = amplitude[:, lanes] * jnp.minimum(
+            lax.rsqrt(real * real + imag * imag), 1.0 / MODULUS_FLOOR)
+        waves[:, lanes] = times_left(
+            tables[2], tables[3], jnp.concatenate([real * factor, imag * factor], axis=0))
+
+    def backward_rows(t):
+        cols = pl.ds(t * tile, tile)
         stacked = []
-        for k in range(len(pair)):
-            block = back[:, k * frame : (k + 1) * frame]
-            stacked.append(jnp.concatenate([block[:frame], block[frame:]], axis=1))
-        return times_right(jnp.concatenate(stacked, axis=0), a_high, a_low)
+        for j in range(frames):
+            lanes = pl.ds(j * frame, frame)
+            stacked.append(jnp.concatenate(
+                [waves[cols, lanes], waves[pl.ds(frame + t * tile, tile), lanes]], axis=1))
+        out = times_right(jnp.concatenate(stacked, axis=0), tables[0], tables[1])
+        back_real, back_imag = [], []
+        for j in range(frames):
+            block = out[j * tile : (j + 1) * tile]
+            real, imag = block[:, :frame], block[:, frame:]
+            p_real, p_imag = rolled[j, 0, cols, :], rolled[j, 1, cols, :]
+            back_real.append(p_real * real + p_imag * imag)
+            back_imag.append(p_real * imag - p_imag * real)
+        for channel, pieces in enumerate((back_real, back_imag)):
+            for target, value in unfold(t, pieces):
+                summed[channel, pl.ds(target * tile, tile), :] = value
+
+    order = sorted(range(1, bands - 1), key=lambda t: -abs(t - reach))
 
     def iterate(iteration, carry):
         for t in offsets:
             est_copy(t).start()
+        for t in reversed(order):
+            if t != reach:
+                est_copy(t).wait()
+            forward_rows(t)
+        for t in (0, bands - 1):
+            est_copy(t).wait()
+
+        @pl.when(iteration == 0)
+        def _():
+            for t in offsets:
+                cover_copy(t).start()
+
+        forward_rows(0)
+        step = 2 if frames % 2 == 0 else 1
+        for begin in range(0, frames, step):
+            correct(begin, step)
+        backward_rows(0)
+        for t in (0, bands - 1):
+            sum_copy(t).start()
+        for t in order:
+            backward_rows(t)
+            if t != reach:
+                sum_copy(t).start()
 
         @pl.when(iteration == 0)
         def _():
@@ -238,20 +272,6 @@
                 total = total + cover_in[t]
             inverse[...] = 1.0 / (total + INTERSECTION_WEIGHT)
 
-        for t in offsets:
-            est_copy(t).wait()
-        step = 2 if frames % 2 == 0 else 1
-        for begin in range(0, frames, step):
-            pair = list(range(begin, begin + step))
-            out = transform_pair(pair)
-            for k, j in enumerate(pair):
-                block = out[k * frame : (k + 1) * frame]
-                real, imag = block[:, :frame], block[:, frame:]
-                p_real, p_imag = rolled[j, 0], rolled[j, 1]
-                unfold(j, p_real * real + p_imag * imag, summed, 0, j == 0)
-                unfold(j, p_real * imag - p_imag * real, summed, 1, j == 0)
-        for t in offsets:
-            sum_copy(t).start()
         for t in offsets:
             sum_copy(t).wait()
         for channel in range(2):
@@ -346,7 +366,7 @@
         scratch_shapes=[
             pltpu.VMEM((2, layers, tile, rows), F32),
             pltpu.VMEM((frames, 2, frame, frame), F32),
-            pltpu.VMEM((frames, frame, frame), F32),
+            pltpu.VMEM((frame, frames * frame), F32),
             pltpu.VMEM((bands * tile, rows), F32),
             pltpu.VMEM((bands, tile, rows), F32),
             pltpu.VMEM((tile, rows), F32),
@@ -356,6 +376,7 @@
             pltpu.VMEM((2, bands * tile, rows), F32),
             pltpu.VMEM((2, bands * tile, rows), F32),
             pltpu.VMEM((bands, 2, tile, rows), F32),
+            pltpu.VMEM((2 * frame, frames * frame), F32),
             dma,
             dma((bands,)), dma((bands,)), dma((2,)), dma((2,)), dma((bands,)), dma((bands,)),
             dma((bands,)), dma((bands,)), dma((2,)), dma((2,)), dma((n_ang,)), dma((n_ang,)),
@@ -363,7 +384,7 @@
         ],
         compiler_params=pltpu.CompilerParams(collective_id=0, has_side_effects=True),
         name="update",
-    )(positions, shear_steps, object_field, probe_wave, intensity[0], tables)
+    )(positions.T, shear_steps, object_field, probe_wave, intensity[0], tables)
 
     depth = 8 if layers % 8 == 0 else layers
     block = pl.BlockSpec((2, depth, tile, rows), lambda i: (0, i, 0, 0))

time: 69.7 us -> 67.8 us (0.973)
  local copies, waits for them, and re-layouts: 1.34 us -> 0 us
    unnamed x1 -> x0, local copies, waits for them, and re-layouts: 1.34 us -> none
where the time goes in v2:
time: 67.8 us; the launch traced here: 67.6 us
  Pallas kernels  67.6 us (100%)
    pallas_call x1, Pallas kernels, per_device(): pl.pallas_call(functools.partial(update_kernel, n_pos, n_ang), out_shape=...  62.9 us
    pallas_call x1, Pallas kernels, per_device(): pl.pallas_call(functools.partial(spread_kernel, RELAXATION / shear_steps....  4.64 us

profile of v2, /device:TPU:0, one launch (start us, length us, event | category | flops | bytes accessed | tf_op | source)
XLA Modules:
  0.0 67.6 jit_solution(13828258115304088489)
XLA Ops:
  0.0 62.9 %update.1.gathered = f32[4,2,48,256]{3,2,1,0:T(8,128)} custom-call(s32[2,4]{1,0:T(2,128)} %bitcast.3, s32[4,32]{1,0:T(4,128)} %steps.3, f32[2,32,32,256]{3,2,1,0:T(8,128)} %object_block.1, f32[2,128,128]{2,1,0:T(8,128)} %probe.1, f32[4,128,128]{2,1,0:T(8,128)} %bitcast.2, bf16[4,256,256]{2,1,0:T(8,128)(2,1)} %constant.2.clone.tables), custom_call_target="tpu_custom_call" | custom-call | tf_op jit(solution)/shard_map/update/pallas_call | solution.py:361
  62.9 4.6 %spread.1 = f32[2,32,32,256]{3,2,1,0:T(8,128)} custom-call(s32[4,32]{1,0:T(4,128)} %steps.3, f32[2,32,32,256]{3,2,1,0:T(8,128)} %object_block.1, f32[4,2,48,256]{3,2,1,0:T(8,128)} %update.1.gathered), custom_call_target="tpu_custom_call" | custom-call | tf_op jit(solution)/shard_map/spread/pallas_call | solution.py:391

commit v3 on v2

--- a/solution.py
+++ b/solution.py
@@ -16,6 +16,7 @@
 MESH = pl.DeviceIdType.MESH
 F32 = jnp.float32
 BF16 = jnp.bfloat16
+OUT, PAIR, FAR, EXTRA = range(4)
 
 
 def dft_tables(length):
@@ -167,17 +168,25 @@
         first[channel] = value
         source[channel, mine, :] = value
 
-    def est_copy(t):
-        return pltpu.make_async_remote_copy(
-            src_ref=source.at[:, mine, :], dst_ref=source.at[:, pl.ds(t * tile, tile), :],
-            send_sem=est_send.at[t], recv_sem=est_recv.at[t],
-            device_id={"pos": at(reach - t)}, device_id_type=MESH)
-
-    def sum_copy(t):
-        return pltpu.make_async_remote_copy(
-            src_ref=summed.at[:, pl.ds(t * tile, tile), :], dst_ref=sums_in.at[t],
-            send_sem=sum_send.at[t], recv_sem=sum_recv.at[t],
-            device_id={"pos": at(t - reach)}, device_id_type=MESH)
+    out_sign = 2 * lax.rem(me, 2) - 1
+
+    def tile_at(step):
+        return pl.ds(pl.multiple_of((reach + step * out_sign) * tile, tile), tile)
+
+    def est_copy(role):
+        sent, to, landing = (
+            (0, 1, -1), (0, -1, 1), (0, -2, 2), (1, -1, 2))[role]
+        return pltpu.make_async_remote_copy(
+            src_ref=source.at[:, tile_at(sent), :], dst_ref=source.at[:, tile_at(landing), :],
+            send_sem=est_send.at[role], recv_sem=est_recv.at[role],
+            device_id={"pos": at(to * out_sign)}, device_id_type=MESH)
+
+    def sum_copy(role):
+        sent, to = ((1, 1), (-1, -1), (2, 2), (-2, -1))[role]
+        return pltpu.make_async_remote_copy(
+            src_ref=summed.at[:, tile_at(sent), :], dst_ref=sums_in.at[role],
+            send_sem=sum_send.at[role], recv_sem=sum_recv.at[role],
+            device_id={"pos": at(to * out_sign)}, device_id_type=MESH)
 
     def fold(t, channel, j):
         low_half = lane >= row_at[j]
@@ -237,14 +246,19 @@
     order = sorted(range(1, bands - 1), key=lambda t: -abs(t - reach))
 
     def iterate(iteration, carry):
-        for t in offsets:
-            est_copy(t).start()
-        for t in reversed(order):
+        est_copy(OUT).start()
+        est_copy(PAIR).start()
+        forward_rows(reach)
+        est_copy(OUT).wait_send()
+        est_copy(FAR).start()
+        est_copy(OUT).wait_recv()
+        est_copy(EXTRA).start()
+        est_copy(PAIR).wait()
+        for t in order:
             if t != reach:
-                est_copy(t).wait()
-            forward_rows(t)
-        for t in (0, bands - 1):
-            est_copy(t).wait()
+                forward_rows(t)
+        est_copy(FAR).wait()
+        est_copy(EXTRA).wait()
 
         @pl.when(iteration == 0)
         def _():
@@ -256,12 +270,17 @@
         for begin in range(0, frames, step):
             correct(begin, step)
         backward_rows(0)
-        for t in (0, bands - 1):
-            sum_copy(t).start()
+        sum_copy(EXTRA).start()
+        sum_copy(FAR).start()
         for t in order:
-            backward_rows(t)
             if t != reach:
-                sum_copy(t).start()
+                backward_rows(t)
+        sum_copy(PAIR).start()
+        sum_copy(EXTRA).wait()
+        for channel in range(2):
+            summed[channel, tile_at(1), :] += sums_in[EXTRA, channel]
+        sum_copy(OUT).start()
+        backward_rows(reach)
 
         @pl.when(iteration == 0)
         def _():
@@ -272,12 +291,12 @@
                 total = total + cover_in[t]
             inverse[...] = 1.0 / (total + INTERSECTION_WEIGHT)
 
-        for t in offsets:
-            sum_copy(t).wait()
+        for role in (PAIR, FAR, OUT):
+            sum_copy(role).wait()
         for channel in range(2):
             total = summed[channel, mine, :]
-            for t in offsets:
-                total = total + sums_in[t, channel]
+            for role in (PAIR, FAR, OUT):
+                total = total + sums_in[role, channel]
             old = source[channel, mine, :]
             source[channel, mine, :] = (total + INTERSECTION_WEIGHT * old) * inverse[...]
         return carry
@@ -352,7 +371,7 @@
     reach = -(-(frame // 2) // tile)
     bands = 2 * reach + 1
     assert intensity.shape[0] == 1 and frame == 2 * reach * tile and rows == 2 * frame
-    assert n_pos >= bands
+    assert n_pos >= bands and n_pos % 2 == 0 and reach == 2
     tables = jnp.asarray(dft_tables(frame))
     wide = tile + 2 * SH
     vmem = pl.BlockSpec(memory_space=pltpu.VMEM)
@@ -375,11 +394,11 @@
             pltpu.VMEM((2, tile, rows), F32),
             pltpu.VMEM((2, bands * tile, rows), F32),
             pltpu.VMEM((2, bands * tile, rows), F32),
-            pltpu.VMEM((bands, 2, tile, rows), F32),
+            pltpu.VMEM((4, 2, tile, rows), F32),
             pltpu.VMEM((2 * frame, frames * frame), F32),
             dma,
-            dma((bands,)), dma((bands,)), dma((2,)), dma((2,)), dma((bands,)), dma((bands,)),
-            dma((bands,)), dma((bands,)), dma((2,)), dma((2,)), dma((n_ang,)), dma((n_ang,)),
+            dma((bands,)), dma((bands,)), dma((2,)), dma((2,)), dma((4,)), dma((4,)),
+            dma((4,)), dma((4,)), dma((2,)), dma((2,)), dma((n_ang,)), dma((n_ang,)),
             dma((n_ang, 2)), dma((n_ang, 2)),
         ],
         compiler_params=pltpu.CompilerParams(collective_id=0, has_side_effects=True),

time: 67.8 us -> 60.5 us (0.89)
  Pallas kernels: 67.6 us -> 60.3 us
    pallas_call x1, Pallas kernels: 62.9 us -> 55.6 us  [per_device(): pl.pallas_call(functools.partial(update_kernel, n_pos, n_ang), out_shape=...]
where the time goes in v3:
time: 60.5 us; the launch traced here: 60.3 us
  Pallas kernels  60.3 us (100%)
    pallas_call x1, Pallas kernels, per_device(): pl.pallas_call(functools.partial(update_kernel, n_pos, n_ang), out_shape=...  55.6 us
    pallas_call x1, Pallas kernels, per_device(): pl.pallas_call(functools.partial(spread_kernel, RELAXATION / shear_steps....  4.64 us

profile of v3, /device:TPU:0, one launch (start us, length us, event | category | flops | bytes accessed | tf_op | source)
XLA Modules:
  0.0 60.3 jit_solution(9692944643718879517)
XLA Ops:
  0.0 55.6 %update.1.gathered = f32[4,2,48,256]{3,2,1,0:T(8,128)} custom-call(s32[2,4]{1,0:T(2,128)} %bitcast.3, s32[4,32]{1,0:T(4,128)} %steps.3, f32[2,32,32,256]{3,2,1,0:T(8,128)} %object_block.1, f32[2,128,128]{2,1,0:T(8,128)} %probe.1, f32[4,128,128]{2,1,0:T(8,128)} %bitcast.2, bf16[4,256,256]{2,1,0:T(8,128)(2,1)} %constant.2.clone.tables), custom_call_target="tpu_custom_call" | custom-call | tf_op jit(solution)/shard_map/update/pallas_call | solution.py:380
  55.6 4.6 %spread.1 = f32[2,32,32,256]{3,2,1,0:T(8,128)} custom-call(s32[4,32]{1,0:T(4,128)} %steps.3, f32[2,32,32,256]{3,2,1,0:T(8,128)} %object_block.1, f32[4,2,48,256]{3,2,1,0:T(8,128)} %update.1.gathered), custom_call_target="tpu_custom_call" | custom-call | tf_op jit(solution)/shard_map/spread/pallas_call | solution.py:410

commit v4 on v3

--- a/solution.py
+++ b/solution.py
@@ -327,7 +327,7 @@
 
     for side in range(2):
         edge_copy(side).start()
-    for d in range(1, n_ang):
+    for d in sorted(range(1, n_ang), key=lambda d: -min(d, n_ang - d)):
         core_copy(d, ang).start()
     for side in range(2):
         edge_copy(side).wait()
@@ -346,17 +346,15 @@
     _, depth, tile, rows = object_block.shape
     n_ang, _, wide, _ = gathered.shape
     first_layer = pl.program_id(0) * depth
-    lane = lax.broadcasted_iota(jnp.int32, (tile, n_ang * wide), 1)
-    offset = lane - lax.broadcasted_iota(jnp.int32, (tile, n_ang * wide), 0)
+    offset = lax.broadcasted_iota(jnp.int32, (tile, n_ang * wide), 1) - lax.broadcasted_iota(
+        jnp.int32, (tile, n_ang * wide), 0)
+    lane = lax.broadcasted_iota(jnp.int32, (1, n_ang * wide), 1)
     blocks = []
     for z in range(depth):
-        chosen = None
-        for a in range(n_ang):
-            begin = a * wide
-            inside = (lane >= begin) & (lane < begin + wide)
-            hit = inside & (offset == begin + SH - steps[a, first_layer + z])
-            chosen = hit if chosen is None else chosen | hit
-        blocks.append(jnp.where(chosen, 1.0, 0.0))
+        target = jnp.full((1, n_ang * wide), SH - steps[0, first_layer + z], jnp.int32)
+        for a in range(1, n_ang):
+            target = jnp.where(lane >= a * wide, a * wide + SH - steps[a, first_layer + z], target)
+        blocks.append(jnp.where(offset == target, 1.0, 0.0))
     pick = jnp.concatenate(blocks, axis=0).astype(BF16)
     for channel in range(2):
         high, low = split(gathered[:, channel].reshape(n_ang * wide, rows))

time: 60.5 us -> 60.3 us (level)
  no operation moved by 1% of the time
where the time goes in v4:
time: 60.3 us; the launch traced here: 60.1 us
  Pallas kernels  60.1 us (100%)
    pallas_call x1, Pallas kernels, per_device(): pl.pallas_call(functools.partial(update_kernel, n_pos, n_ang), out_shape=...  55.6 us
    pallas_call x1, Pallas kernels, per_device(): pl.pallas_call(functools.partial(spread_kernel, RELAXATION / shear_steps....  4.49 us

profile of v4, /device:TPU:0, one launch (start us, length us, event | category | flops | bytes accessed | tf_op | source)
XLA Modules:
  0.0 60.1 jit_solution(14326587231062440432)
XLA Ops:
  0.0 55.6 %update.1.gathered = f32[4,2,48,256]{3,2,1,0:T(8,128)} custom-call(s32[2,4]{1,0:T(2,128)} %bitcast.3, s32[4,32]{1,0:T(4,128)} %steps.3, f32[2,32,32,256]{3,2,1,0:T(8,128)} %object_block.1, f32[2,128,128]{2,1,0:T(8,128)} %probe.1, f32[4,128,128]{2,1,0:T(8,128)} %bitcast.2, bf16[4,256,256]{2,1,0:T(8,128)(2,1)} %constant.2.clone.tables), custom_call_target="tpu_custom_call" | custom-call | tf_op jit(solution)/shard_map/update/pallas_call | solution.py:378
  55.6 4.5 %spread.1 = f32[2,32,32,256]{3,2,1,0:T(8,128)} custom-call(s32[4,32]{1,0:T(4,128)} %steps.3, f32[2,32,32,256]{3,2,1,0:T(8,128)} %object_block.1, f32[4,2,48,256]{3,2,1,0:T(8,128)} %update.1.gathered), custom_call_target="tpu_custom_call" | custom-call | tf_op jit(solution)/shard_map/spread/pallas_call | solution.py:408

commit v5 on v4

--- a/solution.py
+++ b/solution.py
@@ -403,7 +403,7 @@
         name="update",
     )(positions.T, shear_steps, object_field, probe_wave, intensity[0], tables)
 
-    depth = 8 if layers % 8 == 0 else layers
+    depth = 16 if layers % 16 == 0 else layers
     block = pl.BlockSpec((2, depth, tile, rows), lambda i: (0, i, 0, 0))
     return pl.pallas_call(
         functools.partial(spread_kernel, RELAXATION / shear_steps.shape[0]),

time: 60.3 us -> 59.1 us (0.980)
  Pallas kernels: 60.1 us -> 58.9 us
    pallas_call x1, Pallas kernels: 4.49 us -> 3.26 us  [per_device(): pl.pallas_call(functools.partial(spread_kernel, RELAXATION / shear_steps....]
where the time goes in v5:
time: 59.1 us; the launch traced here: 58.9 us
  Pallas kernels  58.9 us (100%)
    pallas_call x1, Pallas kernels, per_device(): pl.pallas_call(functools.partial(update_kernel, n_pos, n_ang), out_shape=...  55.6 us
    pallas_call x1, Pallas kernels, per_device(): pl.pallas_call(functools.partial(spread_kernel, RELAXATION / shear_steps....  3.26 us

profile of v5, /device:TPU:0, one launch (start us, length us, event | category | flops | bytes accessed | tf_op | source)
XLA Modules:
  0.0 58.9 jit_solution(2859130964449249574)
XLA Ops:
  0.0 55.6 %update.1.gathered = f32[4,2,48,256]{3,2,1,0:T(8,128)} custom-call(s32[2,4]{1,0:T(2,128)} %bitcast.3, s32[4,32]{1,0:T(4,128)} %steps.3, f32[2,32,32,256]{3,2,1,0:T(8,128)} %object_block.1, f32[2,128,128]{2,1,0:T(8,128)} %probe.1, f32[4,128,128]{2,1,0:T(8,128)} %bitcast.2, bf16[4,256,256]{2,1,0:T(8,128)(2,1)} %constant.2.clone.tables), custom_call_target="tpu_custom_call" | custom-call | tf_op jit(solution)/shard_map/update/pallas_call | solution.py:378
  55.6 3.3 %spread.1 = f32[2,32,32,256]{3,2,1,0:T(8,128)} custom-call(s32[4,32]{1,0:T(4,128)} %steps.3, f32[2,32,32,256]{3,2,1,0:T(8,128)} %object_block.1, f32[4,2,48,256]{3,2,1,0:T(8,128)} %update.1.gathered), custom_call_target="tpu_custom_call" | custom-call | tf_op jit(solution)/shard_map/spread/pallas_call | solution.py:408
